TPU v7x, 256 devices: a whole 4x4x8 slice. The times are simulated.
256 devices in a mesh: gx: 64 (over x, z, core), af: 4 (over y).
Axes of the slice: x: 4, y: 4, z: 8, core: 2. Of those that a mesh axis runs over, the one named last changes fastest.
Arguments:
- scalar_field: float32 [128, 512, 512], P('gx', 'af'), may hold values from -256 to 256
- plane_sketch: float32 [128, 2, 256], P('gx'), may hold values from -0.5 to 0.5
- second_sketch: float32 [512, 256], P('af'), may hold values from -0.25 to 0.25
- third_sketch: float32 [512, 256], replicated, may hold values from -0.25 to 0.25
- mixing: float32 [2, 256, 128], replicated, may hold values from -0.375 to 0.375
- plane_targets: int32 [128, 2], replicated, may hold values from 0 to 7
- plane_signs: int32 [128, 2], replicated, may hold values from 0 to 1
Outputs:
- factor_second: float32 [512, 128], P(('af', 'gx'))
- factor_third: float32 [512, 128], P(('gx', 'af'))
- core_sketch: float32 [128, 128, 128], P('gx', 'af')
Inputs may be any that keep to these rules, and one draw needn't show every extreme that they name: `plane_targets`: block id of each of a plane's two entries in the core sketch; the two may coincide. `plane_signs`: 1 stands for a plus sign, 0 for a minus sign.
All inputs are finite; a program needn't handle non-finite values.
Results may differ from a plain program's by a relative error of at most 0.0003.
Values sent between devices are 32-bit elements; how exact they have to be, the bound alone decides.
A program may use at most 64 MiB of HBM per device.

v0:
```python
import jax
import jax.numpy as jnp
from jax import lax
from jax.sharding import PartitionSpec as P

BLOCK = 16
BLOCKS = 8
precise = lax.Precision.HIGHEST


def gram_of(ranged):
    return jnp.dot(ranged.T, ranged, precision=precise)


def orthonormal_rows(ranged, gram_matrix):
    lower_factor = jnp.linalg.cholesky(gram_matrix)
    return jax.scipy.linalg.solve_triangular(lower_factor, ranged.T, lower=True).T


def selector(targets, sign_values, row_count):
    row_ids = jnp.arange(row_count, dtype=jnp.int32)
    return jnp.sum(
        jnp.where(targets[None, :, :] == row_ids[:, None, None], sign_values[None, :, :], 0.0),
        axis=2,
    )


def body(
    scalar_field, plane_sketch, second_sketch, third_sketch, mixing, plane_targets, plane_signs
):
    planes = scalar_field.shape[0]
    rank_cols = mixing.shape[2]
    along_second = jnp.einsum("pjl,lk->pjk", scalar_field, third_sketch, precision=precise)
    partial_second = jnp.einsum(
        "pjk,pk->jk", along_second, plane_sketch[:, 0, :], precision=precise
    )
    along_third = jnp.einsum("pjl,jk->plk", scalar_field, second_sketch, precision=precise)
    partial_third = jnp.einsum("plk,pk->lk", along_third, plane_sketch[:, 1, :], precision=precise)

    def finish(sketched, mode_index):
        return jnp.dot(sketched, mixing[mode_index], precision=precise)

    rows_second = finish(lax.psum_scatter(partial_second, "gx", scatter_dimension=0, tiled=True), 0)
    rows_third = finish(
        lax.psum_scatter(partial_third, ("gx", "af"), scatter_dimension=0, tiled=True), 1
    )
    gram_second, gram_third = lax.psum((gram_of(rows_second), gram_of(rows_third)), ("gx", "af"))
    factor_second = orthonormal_rows(rows_second, gram_second)
    factor_third = orthonormal_rows(rows_third, gram_third)
    basis_second = lax.all_gather(factor_second, "gx", axis=0, tiled=True)
    basis_third = lax.all_gather(factor_third, ("gx", "af"), axis=0, tiled=True)
    left_side = jnp.einsum("jr,pjl->prl", basis_second, scalar_field, precision=precise)
    projected = jnp.einsum("prl,ls->prs", left_side, basis_third, precision=precise)
    out_rows = BLOCKS * BLOCK // lax.axis_size("gx")
    plane_ids = jnp.arange(plane_targets.shape[0], dtype=jnp.int32)
    all_targets = plane_targets * BLOCK + (plane_ids % BLOCK)[:, None]
    all_signs = (2 * plane_signs - 1).astype(jnp.float32)
    first_plane = lax.axis_index("gx") * planes
    own_targets = lax.dynamic_slice_in_dim(all_targets, first_plane, planes, 0)
    own_signs = lax.dynamic_slice_in_dim(all_signs, first_plane, planes, 0)
    flattened = projected.reshape(planes, -1)
    select = selector(own_targets, own_signs, lax.axis_size("gx") * out_rows)
    partial_core = lax.psum_scatter(
        jnp.dot(select, flattened, precision=precise).reshape(
            lax.axis_size("gx") * out_rows, rank_cols, rank_cols
        ),
        "gx",
        scatter_dimension=0,
        tiled=True,
    )
    core_sketch = lax.psum_scatter(partial_core, "af", scatter_dimension=1, tiled=True)
    return (factor_second, factor_third, core_sketch)


def solution(mesh):
    in_specs = (P("gx", "af", None), P("gx", None, None), P("af", None), P(), P(), P(), P())
    out_specs = (P(("af", "gx"), None), P(("gx", "af"), None), P("gx", "af", None))
    return jax.shard_map(body, mesh=mesh, in_specs=in_specs, out_specs=out_specs, check_vma=False)
```

profile of v0, /device:TPU:2, one launch (start us, length us, event | category | flops | bytes accessed | tf_op | source)
XLA Modules:
  0.0 1100.5 jit_solution(13940723075682379421)
XLA Ops:
  7.2 0.8 fusion.30
  8.0 0.2 copy-done
  8.2 1.6 fusion.3
  9.9 0.8 copy.63
  10.7 0.0 all-reduce.11.cloned.1.call-start
  10.7 2.0 fusion.1
  12.7 1.0 copy.72
  13.8 1.3 dynamic-slice
  15.7 0.7 multiply_add_fusion
  16.4 0.1 constant_dynamic-slice_fusion.2
  16.5 0.1 copy.51
  16.6 0.7 add_convert_fusion
  17.3 0.1 constant_dynamic-slice_fusion.1
  17.4 0.1 copy.52
  17.5 168.7 %all-reduce.9.cloned.1.call-done = f32[128,256]{0,1:T(8,128)} async-done(((f32[128,256]{0,1:T(8,128)}), f32[128,256]{0,1:T(8,128)}) %all-reduce.9.cloned.1.call-update) | async-done | bytes 131088
  186.2 1.4 fusion.9
  187.6 0.9 fusion.31
  188.5 254.2 %all-reduce.11.cloned.1.call-done = f32[512,256]{0,1:T(8,128)} async-done(((f32[512,256]{0,1:T(8,128)}), f32[512,256]{0,1:T(8,128)}) %all-reduce.11.cloned.1.call-update) | async-done | bytes 524304
  442.7 1.4 fusion.7
  444.1 0.9 fusion.32
  445.1 0.1 fusion.24
  445.2 243.7 %all-reduce.15.cloned.1.call-done = (f32[128,128]{0,1:T(8,128)}, f32[128,128]{0,1:T(8,128)}) async-done(((f32[128,128]{0,1:T(8,128)}, f32[128,128]{0,1:T(8,128)}), (f32[128,128]{0,1:T(8,128)}, f32[128,128]{0,1:T(8,128)})) %all-reduce.15.cloned.1.call-update) | async-done | bytes 131088 | tf_op jit(solution)/shard_map/psum | solution.py:47
  688.9 0.9 copy.47
  689.9 0.9 fusion.23
  690.7 11.7 %cholesky.44 = f32[128,128]{1,0:T(8,128)S(1)} custom-call(f32[128,128]{1,0:T(8,128)S(1)} %fusion.23), custom_call_target="Cholesky" | custom-call | tf_op jit(solution)/shard_map/jit(cholesky)/cholesky | solution.py:16
  702.5 0.6 compare_reduce_fusion.1
  703.1 0.7 fusion.16
  703.8 9.8 custom-call.6
  713.6 0.2 fusion.21
  713.7 41.4 %all-gather = f32[64,2,128]{2,1,0:T(2,128)S(1)} all-gather(f32[1,2,128]{2,1,0:T(2,128)S(1)} %bitcast.107), channel_id=1, replica_groups=mesh['gx'=64,'af'=4] {'gx'}, dimensions={0}, use_global_device_ids=true | all-gather | bytes 66560 | tf_op jit(solution)/shard_map/all_gather | solution.py:50
  755.2 0.9 copy.50
  756.1 0.9 fusion.20
  757.0 11.7 %cholesky.55 = f32[128,128]{1,0:T(8,128)S(1)} custom-call(f32[128,128]{1,0:T(8,128)S(1)} %fusion.20), custom_call_target="Cholesky" | custom-call | tf_op jit(solution)/shard_map/jit(cholesky)/cholesky | solution.py:16
  768.7 0.6 compare_reduce_fusion
  769.4 0.7 fusion.17
  770.0 9.8 custom-call.7
  779.8 0.2 fusion.18
  780.0 101.1 %all-gather.1 = f32[256,2,128]{2,1,0:T(2,128)S(1)} all-gather(f32[1,2,128]{2,1,0:T(2,128)S(1)} %bitcast.109), channel_id=1, replica_groups=mesh['gx'=64,'af'=4] {'gx','af'}, dimensions={0}, use_global_device_ids=true | all-gather | bytes 263168 | tf_op jit(solution)/shard_map/all_gather | solution.py:51
  881.1 0.6 convolution_bitcast_fusion.1
  881.7 0.6 convolution_bitcast_fusion.3
  882.3 6.8 fusion.5
  889.1 8.1 copy.54
  897.3 147.7 %reduce-scatter.4.cloned.1.call-done = f32[2,128,128]{2,1,0:T(8,128)} async-done(((f32[128,128,128]{2,1,0:T(8,128)}), f32[2,128,128]{2,1,0:T(8,128)}) %reduce-scatter.4.cloned.1.call-update) | async-done | bytes 131088 | tf_op jit(solution)/shard_map/reduce_scatter | solution.py:63
  1044.9 1.6 copy.55
  1046.6 0.6 dynamic-slice.3
  1047.9 44.8 %all-reduce.13.cloned.1.call-done = f32[2,128,128]{2,0,1:T(2,128)} async-done(((f32[2,128,128]{2,0,1:T(2,128)}), f32[2,128,128]{2,0,1:T(2,128)}) %all-reduce.13.cloned.1.call-update) | async-done | bytes 131088
  1092.6 0.8 constant_dynamic-slice_fusion
  1093.4 0.6 copy.56
  (20 shorter events, 0.3 us)
Async XLA Ops:
  7.2 1.1 copy-start
  7.2 179.0 %all-reduce.9.cloned.1.call-start = ((), (), s32[]{:S(2)}) async-start(), calls=%async_computation.2 | async-start | bytes 262144
  10.7 432.0 %all-reduce.11.cloned.1.call-start = ((), (), s32[]{:S(2)}) async-start(), calls=%async_computation.3 | async-start | bytes 1048576
  13.7 675.2 %all-reduce.15.cloned.1.call-start = ((), (), s32[]{:S(2)}) async-start(), calls=%async_computation.5 | async-start | bytes 262144 | tf_op jit(solution)/shard_map/psum | solution.py:47
  445.1 599.9 %reduce-scatter.4.cloned.1.call-start = ((), (), s32[]{:S(2)}) async-start(), calls=%async_computation.1 | async-start | bytes 8519680 | tf_op jit(solution)/shard_map/reduce_scatter | solution.py:63
  713.7 183.4 %copy-start.1 = (f32[128,2]{0,1:T(2,128)}, f32[128,2]{0,1:T(2,128)S(1)}, u32[]{:S(2)}) copy-start(f32[128,2]{0,1:T(2,128)S(1)} %fusion.21) | copy-start | bytes 3076
  780.0 117.2 %copy-start.2 = (f32[128,2]{0,1:T(2,128)}, f32[128,2]{0,1:T(2,128)S(1)}, u32[]{:S(2)}) copy-start(f32[128,2]{0,1:T(2,128)S(1)} %fusion.18) | copy-start | bytes 3076
  897.2 149.4 %copy-start.3 = (u32[256]{0:T(256)S(1)}, u32[256]{0:T(256)}, u32[]{:S(2)}) copy-start(u32[256]{0:T(256)} %constant.78) | copy-start | bytes 3076
  897.2 195.4 %all-reduce.13.cloned.1.call-start = ((), (), s32[]{:S(2)}) async-start(), calls=%async_computation.4 | async-start | bytes 262144
Sparse Core Ops, SparseCore 0:
  11.5 174.6 all-reduce.8
  191.6 251.0 all-reduce.10
  448.3 240.5 all-reduce.14
  897.3 147.5 reduce-scatter.3
  1047.2 45.3 all-reduce.12
where the time goes:
time: 1100 us
  waiting for transfers between devices  859 us (78%)
  blocking collectives  143 us (13%)
  other arithmetic  48.9 us (4%)
  local copies, waits for them, and re-layouts  17.9 us (2%)
  matrix products  16.6 us (2%)
  between operations  15.2 us (1%)
    unnamed x8, waiting for transfers between devices  468 us
    psum x1, waiting for transfers between devices, body(): lax.psum((gram_of(rows_second), gram_of(rows_third)), ('gx', 'af'))  244 us
    reduce_scatter x1, waiting for transfers between devices, body(): lax.psum_scatter(jnp.dot(select, flattened, precision=precise).reshape(la...  148 us
    all_gather x1, blocking collectives, body(): basis_third = lax.all_gather(factor_third, ('gx', 'af'), axis=0, tiled=True)  101 us
    all_gather x1, blocking collectives, body(): basis_second = lax.all_gather(factor_second, 'gx', axis=0, tiled=True)  41.4 us
    another operation x6, other arithmetic, orthonormal_rows(): lower_factor = jnp.linalg.cholesky(gram_matrix)  24.8 us
  transfers between devices with their start and end apart: 5, of which 5 were waited for; matrix products, arithmetic and copies ran while one was open for 1% of the time, Pallas kernels for 0%

commit v1 on v0

--- a/solution.py
+++ b/solution.py
@@ -48,7 +48,10 @@
     factor_second = orthonormal_rows(rows_second, gram_second)
     factor_third = orthonormal_rows(rows_third, gram_third)
     basis_second = lax.all_gather(factor_second, "gx", axis=0, tiled=True)
-    basis_third = lax.all_gather(factor_third, ("gx", "af"), axis=0, tiled=True)
+    basis_third = jnp.concatenate(
+        lax.all_to_all(jnp.stack([factor_third] * lax.axis_size(("gx", "af"))), ("gx", "af"), 0, 0),
+        axis=0,
+    )
     left_side = jnp.einsum("jr,pjl->prl", basis_second, scalar_field, precision=precise)
     projected = jnp.einsum("prl,ls->prs", left_side, basis_third, precision=precise)
     out_rows = BLOCKS * BLOCK // lax.axis_size("gx")

time: 1100 us -> 1010 us (0.918)
  blocking collectives: 143 us -> 44.9 us
    all_gather x1 -> x0, blocking collectives: 101 us -> none  [body(): basis_third = lax.all_gather(factor_third, ('gx', 'af'), axis=0, tiled=True)]
  transfers between devices with their start and end apart: 5 -> 6, of which waited for: 5 -> 5; matrix products, arithmetic and copies ran while one was open for 1% -> 2% of each run, Pallas kernels for 0% -> 0%
where the time goes in v1:
time: 1010 us
  waiting for transfers between devices  861 us (85%)
  other arithmetic  48.9 us (5%)
  blocking collectives  44.9 us (4%)
  local copies, waits for them, and re-layouts  18.7 us (2%)
  matrix products  16.6 us (2%)
  between operations  15.2 us (2%)
    unnamed x8, waiting for transfers between devices  468 us
    psum x1, waiting for transfers between devices, body(): lax.psum((gram_of(rows_second), gram_of(rows_third)), ('gx', 'af'))  244 us
    reduce_scatter x1, waiting for transfers between devices, body(): lax.psum_scatter(jnp.dot(select, flattened, precision=precise).reshape(la...  149 us
    all_gather x1, blocking collectives, body(): basis_second = lax.all_gather(factor_second, 'gx', axis=0, tiled=True)  44.9 us
    another operation x6, other arithmetic, orthonormal_rows(): lower_factor = jnp.linalg.cholesky(gram_matrix)  24.8 us
    another operation x4, other arithmetic, orthonormal_rows(): jax.scipy.linalg.solve_triangular(lower_factor, ranged.T, lower=True)  20.9 us
  transfers between devices with their start and end apart: 6, of which 5 were waited for; matrix products, arithmetic and copies ran while one was open for 2% of the time, Pallas kernels for 0%

profile of v1, /device:TPU:2, one launch (start us, length us, event | category | flops | bytes accessed | tf_op | source)
XLA Modules:
  0.0 1014.0 jit_solution(18358647308889119063)
XLA Ops:
  7.2 0.8 fusion.29
  8.0 0.2 copy-done
  8.2 1.6 fusion.3
  9.9 0.8 copy.63
  10.7 2.0 fusion.1
  12.7 1.0 copy.72
  13.8 1.3 dynamic-slice
  15.7 0.7 multiply_add_fusion
  16.4 0.1 constant_dynamic-slice_fusion.2
  16.5 0.1 copy.51
  16.6 0.7 add_convert_fusion
  17.3 0.1 constant_dynamic-slice_fusion.1
  17.4 0.1 copy.52
  17.5 168.7 %all-reduce.9.cloned.1.call-done = f32[128,256]{0,1:T(8,128)} async-done(((f32[128,256]{0,1:T(8,128)}), f32[128,256]{0,1:T(8,128)}) %all-reduce.9.cloned.1.call-update) | async-done | bytes 131088
  186.2 1.4 fusion.9
  187.6 0.9 fusion.30
  188.5 254.2 %all-reduce.11.cloned.1.call-done = f32[512,256]{0,1:T(8,128)} async-done(((f32[512,256]{0,1:T(8,128)}), f32[512,256]{0,1:T(8,128)}) %all-reduce.11.cloned.1.call-update) | async-done | bytes 524304
  442.7 1.4 fusion.7
  444.1 0.9 fusion.31
  445.1 0.1 fusion.23
  445.2 243.8 %all-reduce.15.cloned.1.call-done = (f32[128,128]{0,1:T(8,128)}, f32[128,128]{0,1:T(8,128)}) async-done(((f32[128,128]{0,1:T(8,128)}, f32[128,128]{0,1:T(8,128)}), (f32[128,128]{0,1:T(8,128)}, f32[128,128]{0,1:T(8,128)})) %all-reduce.15.cloned.1.call-update) | async-done | bytes 131088 | tf_op jit(solution)/shard_map/psum | solution.py:47
  688.9 0.9 copy.47
  689.9 0.9 fusion.22
  690.7 11.7 %cholesky.44 = f32[128,128]{1,0:T(8,128)S(1)} custom-call(f32[128,128]{1,0:T(8,128)S(1)} %fusion.22), custom_call_target="Cholesky" | custom-call | tf_op jit(solution)/shard_map/jit(cholesky)/cholesky | solution.py:16
  702.5 0.6 compare_reduce_fusion.1
  703.1 0.9 copy.50
  704.0 0.9 fusion.19
  704.9 11.7 %cholesky.55 = f32[128,128]{1,0:T(8,128)S(1)} custom-call(f32[128,128]{1,0:T(8,128)S(1)} %fusion.19), custom_call_target="Cholesky" | custom-call | tf_op jit(solution)/shard_map/jit(cholesky)/cholesky | solution.py:16
  716.6 0.6 compare_reduce_fusion
  717.3 0.7 fusion.17
  717.9 9.8 custom-call.7
  727.8 0.2 convolution_bitcast_fusion.4
  727.9 0.8 stack.2
  728.7 8.5 all-to-all-start
  737.2 0.7 fusion.16
  737.9 9.8 custom-call.6
  747.7 0.2 fusion.20
  747.9 44.9 %all-gather = f32[64,2,128]{2,1,0:T(2,128)S(1)} all-gather(f32[1,2,128]{2,1,0:T(2,128)S(1)} %bitcast.106), channel_id=1, replica_groups=mesh['gx'=64,'af'=4] {'gx'}, dimensions={0}, use_global_device_ids=true | all-gather | bytes 66560 | tf_op jit(solution)/shard_map/all_gather | solution.py:50
  792.8 0.6 convolution_bitcast_fusion.1
  793.4 0.6 convolution_bitcast_fusion.3
  794.0 6.8 fusion.5
  800.8 8.1 copy.54
  808.9 149.5 %reduce-scatter.4.cloned.1.call-done = f32[2,128,128]{2,1,0:T(8,128)} async-done(((f32[128,128,128]{2,1,0:T(8,128)}), f32[2,128,128]{2,1,0:T(8,128)}) %reduce-scatter.4.cloned.1.call-update) | async-done | bytes 131088 | tf_op jit(solution)/shard_map/reduce_scatter | solution.py:66
  958.4 1.6 copy.55
  960.1 0.6 dynamic-slice.3
  961.3 44.8 %all-reduce.13.cloned.1.call-done = f32[2,128,128]{2,0,1:T(2,128)} async-done(((f32[2,128,128]{2,0,1:T(2,128)}), f32[2,128,128]{2,0,1:T(2,128)}) %all-reduce.13.cloned.1.call-update) | async-done | bytes 131088
  1006.1 0.8 constant_dynamic-slice_fusion
  1006.8 0.6 copy.56
  (22 shorter events, 0.4 us)
Async XLA Ops:
  7.2 1.1 copy-start
  7.2 179.0 %all-reduce.9.cloned.1.call-start = ((), (), s32[]{:S(2)}) async-start(), calls=%async_computation.3 | async-start | bytes 262144
  10.7 432.0 %all-reduce.11.cloned.1.call-start = ((), (), s32[]{:S(2)}) async-start(), calls=%async_computation.4 | async-start | bytes 1048576
  13.7 675.2 %all-reduce.15.cloned.1.call-start = ((), (), s32[]{:S(2)}) async-start(), calls=%async_computation.6 | async-start | bytes 262144 | tf_op jit(solution)/shard_map/psum | solution.py:47
  727.9 80.9 %copy-start.1 = (f32[2,128]{1,0:T(2,128)}, f32[2,128]{1,0:T(2,128)S(1)}, u32[]{:S(2)}) copy-start(f32[2,128]{1,0:T(2,128)S(1)} %convolution_bitcast_fusion.4) | copy-start | bytes 3076
  728.7 64.7 %all-to-all-start = ((f32[256,2,128]{2,1,0:T(2,128)}), f32[256,2,128]{2,1,0:T(2,128)S(1)}, u32[]{:S(2)}, u32[]{:S(2)}) async-start(f32[256,2,128]{2,1,0:T(2,128)} %stack.2), calls=%async_computation | async-start | bytes 524288 | tf_op jit(solution)/shard_map/all_to_all | solution.py:52
  737.2 221.2 %reduce-scatter.4.cloned.1.call-start = ((), (), s32[]{:S(2)}) async-start(), calls=%async_computation.2 | async-start | bytes 8519680 | tf_op jit(solution)/shard_map/reduce_scatter | solution.py:66
  747.9 61.0 %copy-start.2 = (f32[128,2]{0,1:T(2,128)}, f32[128,2]{0,1:T(2,128)S(1)}, u32[]{:S(2)}) copy-start(f32[128,2]{0,1:T(2,128)S(1)} %fusion.20) | copy-start | bytes 3076
  808.9 151.2 %copy-start.3 = (u32[256]{0:T(256)S(1)}, u32[256]{0:T(256)}, u32[]{:S(2)}) copy-start(u32[256]{0:T(256)} %constant.78) | copy-start | bytes 3076
  808.9 197.2 %all-reduce.13.cloned.1.call-start = ((), (), s32[]{:S(2)}) async-start(), calls=%async_computation.5 | async-start | bytes 262144
Sparse Core Ops, SparseCore 0:
  11.5 174.6 all-reduce.8
  191.6 251.0 all-reduce.10
  448.3 240.5 all-reduce.14
  809.0 149.3 reduce-scatter.3
  960.7 45.3 all-reduce.12
